TPU v7x, 512 devices: a whole 4x8x8 slice. The times are simulated.
512 devices in a mesh: round: 128 (over z, y, core), mp: 4 (over x).
Axes of the slice: x: 4, y: 8, z: 8, core: 2. Of those that a mesh axis runs over, the one named last changes fastest.
Arguments:
- tokens: bfloat16 [128, 512, 512], P('round'), may hold values from -8 to 8
- cell_order: int32 [512], replicated, may hold values from 0 to 511, each once
- seam_rows: int32 [128, 128, 2], P('round'), may hold values from -1 to 511, as said below
- obs_mask: int32 [16, 512], replicated, may hold values from 0 to 1, as said below
- norm_gain: float32 [512], replicated, may hold values from 0.1 to 1.9
- w_query: bfloat16 [512, 512], P(None, 'mp'), may hold values from -1 to 1
- w_key: bfloat16 [512, 512], P(None, 'mp'), may hold values from -1 to 1
- w_value: bfloat16 [512, 512], P(None, 'mp'), may hold values from -0.25 to 0.25
- w_out: bfloat16 [512, 512], P('mp'), may hold values from -0.25 to 0.25
- w_gate: bfloat16 [512, 2048], P(None, 'mp'), may hold values from -0.25 to 0.25
- w_up: bfloat16 [512, 2048], P(None, 'mp'), may hold values from -0.25 to 0.25
- w_down: bfloat16 [2048, 512], P('mp'), may hold values from -0.125 to 0.125
- w_read: float32 [512], replicated, may hold values from -0.25 to 0.25
Outputs:
- tiles_out: bfloat16 [128, 512, 512], P('mp', 'round')
- obs_logits: float32 [16], replicated
Inputs may be any that keep to these rules, and one draw needn't show every extreme that they name: `seam_rows`: each entry is a row of the sending tile or -1 for an empty slot; the live entries of one tile are all different; a tile's slots to itself are full, and some owner's slots are full from every tile. `obs_mask`: every observable's support holds at least one cell.
All inputs are finite; a program needn't handle non-finite values.
Results may differ from a plain program's by a relative error of at most 0.0052.
The roundings to bfloat16 on the way count: a program that leaves them out, or rounds other values in their place, can miss the bound.
Values may be sent and summed in bfloat16 or wider, within the bound.
A program may use at most 64 MiB of HBM per device.

v0:
```python
import math

import jax
import jax.numpy as jnp
from jax import lax
from jax.sharding import PartitionSpec as P

HDIM = 64


norm_eps = 1e-06


def normalize(rows_in, norm_gain):
    values = rows_in.astype(jnp.float32)
    spread = jnp.mean(values * values, axis=-1, keepdims=True)
    return (values * lax.rsqrt(spread + norm_eps) * norm_gain).astype(jnp.bfloat16)


def attend(queries, keys_all, values_all, live_keys):
    scale_factor = 1.0 / math.sqrt(queries.shape[-1])
    scores = (
        jnp.einsum("qhe,khe->hqk", queries, keys_all, preferred_element_type=jnp.float32)
        * scale_factor
    )
    if live_keys is not None:
        scores = jnp.where(live_keys[None, None, :], scores, -1e30)
    row_max = jnp.max(scores, axis=-1, keepdims=True)
    weights = jnp.exp(scores - row_max)
    probabilities = (weights / jnp.sum(weights, axis=-1, keepdims=True)).astype(jnp.bfloat16)
    mixture = jnp.einsum(
        "hqk,khe->qhe", probabilities, values_all, preferred_element_type=jnp.float32
    )
    return mixture.reshape(mixture.shape[0], -1)


def shards(
    tokens,
    cell_order,
    seam_rows,
    obs_mask,
    norm_gain,
    w_query,
    w_key,
    w_value,
    w_out,
    w_gate,
    w_up,
    w_down,
    w_read,
):
    round_count = lax.axis_size("round")
    model_count = lax.axis_size("mp")
    model_index = lax.axis_index("mp")
    round_index = lax.axis_index("round")
    width = tokens.shape[2]
    cell_dev = tokens.shape[1] // round_count
    permuted = tokens[:, cell_order, :]
    tile_tokens = lax.all_to_all(permuted, "round", split_axis=1, concat_axis=0, tiled=True)
    tile_rows = tile_tokens.shape[0] * cell_dev
    flat_tokens = tile_tokens.reshape(tile_rows, width)
    normed = normalize(flat_tokens, norm_gain)
    queries = jnp.dot(normed, w_query, preferred_element_type=jnp.float32).astype(jnp.bfloat16)
    keys_all = jnp.dot(normed, w_key, preferred_element_type=jnp.float32).astype(jnp.bfloat16)
    values_all = jnp.dot(normed, w_value, preferred_element_type=jnp.float32).astype(jnp.bfloat16)
    head_width = queries.shape[1]
    heads_dev = head_width // HDIM
    block_rows = min(512, tile_rows)
    query_blocks = queries.reshape(tile_rows // block_rows, block_rows, heads_dev, HDIM)
    key_heads = keys_all.reshape(tile_rows, heads_dev, HDIM)
    value_heads = values_all.reshape(tile_rows, heads_dev, HDIM)
    local_attn = lax.map(
        lambda query_block: attend(query_block, key_heads, value_heads, None), query_blocks
    )
    local_attn = local_attn.reshape(tile_rows, head_width)
    live_slot = seam_rows[0] >= 0
    safe_rows = jnp.where(live_slot, seam_rows[0], 0)
    packet = (
        lax.all_to_all(queries[safe_rows], "round", split_axis=0, concat_axis=0, tiled=True),
        lax.all_to_all(keys_all[safe_rows], "round", split_axis=0, concat_axis=0, tiled=True),
        lax.all_to_all(values_all[safe_rows], "round", split_axis=0, concat_axis=0, tiled=True),
        lax.all_to_all(
            live_slot.astype(jnp.bfloat16), "round", split_axis=0, concat_axis=0, tiled=True
        ),
    )
    seam_queries = packet[0].reshape(-1, heads_dev, HDIM)
    seam_keys = packet[1].reshape(-1, heads_dev, HDIM)
    seam_values = packet[2].reshape(-1, heads_dev, HDIM)
    seam_live = packet[3].reshape(-1) > 0.5
    seam_attn = attend(seam_queries, seam_keys, seam_values, seam_live).astype(jnp.bfloat16)
    returned = lax.all_to_all(
        seam_attn.reshape(round_count, -1, head_width),
        "round",
        split_axis=0,
        concat_axis=0,
        tiled=True,
    )
    target = jnp.where(live_slot, seam_rows[0], tile_rows).reshape(-1)
    combined = (
        local_attn.at[target]
        .add(returned.reshape(-1, head_width).astype(jnp.float32), mode="drop")
        .astype(jnp.bfloat16)
    )
    share_rows = tile_rows // model_count
    own_first = model_index * share_rows
    gate_part = jnp.dot(normed, w_gate, preferred_element_type=jnp.float32)
    up_part = jnp.dot(normed, w_up, preferred_element_type=jnp.float32)
    hidden = (jax.nn.silu(gate_part) * up_part).astype(jnp.bfloat16)
    attn_part = jnp.dot(combined, w_out, preferred_element_type=jnp.float32)
    summed = lax.psum_scatter(
        attn_part + jnp.dot(hidden, w_down, preferred_element_type=jnp.float32),
        "mp",
        scatter_dimension=0,
        tiled=True,
    )
    own_rows = lax.dynamic_slice_in_dim(flat_tokens, own_first, share_rows, 0)
    result_rows = (own_rows.astype(jnp.float32) + summed).astype(jnp.bfloat16)
    tiles_out = result_rows.reshape(share_rows // cell_dev, cell_dev, width)
    my_cells = lax.dynamic_slice_in_dim(cell_order, round_index * cell_dev, cell_dev)
    support = obs_mask[:, my_cells].astype(jnp.float32)
    partial_sum = jnp.einsum(
        "oc,rcd->od", support, tiles_out.astype(jnp.float32), precision=lax.Precision.HIGHEST
    )
    support_count = round_count * jnp.sum(obs_mask.astype(jnp.float32), axis=1)
    divisor = jnp.sqrt(support_count)
    pooled = lax.psum(partial_sum, ("round", "mp"))
    obs_logits = jnp.dot(pooled, w_read, precision=lax.Precision.HIGHEST) / divisor
    return (tiles_out, obs_logits)


def solution(mesh):
    return jax.shard_map(
        shards,
        mesh=mesh,
        in_specs=(
            P("round", None, None),
            P(),
            P("round", None, None),
            P(),
            P(),
            P(None, "mp"),
            P(None, "mp"),
            P(None, "mp"),
            P("mp", None),
            P(None, "mp"),
            P(None, "mp"),
            P("mp", None),
            P(),
        ),
        out_specs=(P("mp", "round", None), P()),
        check_vma=False,
    )
```

profile of v0, /device:TPU:1, one launch (start us, length us, event | category | flops | bytes accessed | tf_op | source)
XLA Modules:
  0.0 291.0 jit_solution(16656046799085090074)
XLA Ops:
  8.7 18.4 %all-to-all-start.2 = ((bf16[128,1,2]{2,1,0:T(2,128)(2,1)}), bf16[128,1,2]{2,1,0:T(2,128)(2,1)S(1)}, u32[]{:S(2)}, u32[]{:S(2)}) async-start(bf16[128,1,2]{2,1,0:T(2,128)(2,1)} %copy.61), calls=%async_computation.2 | async-start | bytes 131072 | tf_op jit(solution)/shard_map/all_to_all | solution.py:82
  27.8 2.0 gather_fusion
  31.1 3.8 %reduce.2 = bf16[512,512]{1,0:T(8,128)(2,1)S(1)} reduce(bf16[512,1,512]{2,1,0:T(2,128)(2,1)S(1)} %bitcast.69, bf16[]{:T(256)} %broadcast.153), dimensions={1}, to_apply=%bitcast.66.reduce_sub_computation | reduce | bytes 1048578
  35.0 1.1 reshape.218
  36.1 2.4 all-to-all-done.2
  38.5 11.3 %all-to-all-start = ((bf16[128,2,1024]{2,1,0:T(2,128)(2,1)}), bf16[128,2,1024]{2,1,0:T(2,128)(2,1)S(1)}, u32[]{:S(2)}, u32[]{:S(2)}) async-start(bf16[128,2,1024]{2,1,0:T(2,128)(2,1)} %reshape.218), calls=%async_computation | async-start | bytes 1048576 | tf_op jit(solution)/shard_map/all_to_all | solution.py:59
  50.8 19.6 %all-to-all-done = bf16[128,2,1024]{2,1,0:T(2,128)(2,1)S(1)} async-done(((bf16[128,2,1024]{2,1,0:T(2,128)(2,1)}), bf16[128,2,1024]{2,1,0:T(2,128)(2,1)S(1)}, u32[]{:S(2)}, u32[]{:S(2)}) %all-to-all-start) | async-done | bytes 524320 | tf_op jit(solution)/shard_map/all_to_all | solution.py:59
  70.9 1.1 bitcast_convert_fusion
  74.1 1.5 gather_fusion.1
  75.6 1.5 gather_fusion.2
  77.0 6.3 %all-to-all-start.3 = ((bf16[128,2,128]{2,1,0:T(2,128)(2,1)}), bf16[128,2,128]{2,1,0:T(2,128)(2,1)}, u32[]{:S(2)}, u32[]{:S(2)}) async-start(bf16[128,2,128]{2,1,0:T(2,128)(2,1)} %bitcast.12), calls=%async_computation.3 | async-start | bytes 131072 | tf_op jit(solution)/shard_map/all_to_all | solution.py:79
  83.3 1.5 fusion.55
  86.8 1.5 gather_fusion.3
  88.3 5.8 %all-to-all-done.3 = bf16[128,2,128]{2,1,0:T(2,128)(2,1)} async-done(((bf16[128,2,128]{2,1,0:T(2,128)(2,1)}), bf16[128,2,128]{2,1,0:T(2,128)(2,1)}, u32[]{:S(2)}, u32[]{:S(2)}) %all-to-all-start.3) | async-done | bytes 65568 | tf_op jit(solution)/shard_map/all_to_all | solution.py:79
  94.1 8.0 %all-to-all-start.4 = ((bf16[128,2,128]{2,1,0:T(2,128)(2,1)}), bf16[128,2,128]{2,1,0:T(2,128)(2,1)}, u32[]{:S(2)}, u32[]{:S(2)}) async-start(bf16[128,2,128]{2,1,0:T(2,128)(2,1)} %bitcast.78), calls=%async_computation.4 | async-start | bytes 131072 | tf_op jit(solution)/shard_map/all_to_all | solution.py:80
  102.1 1.7 fusion.49
  104.8 8.5 %all-to-all-done.4 = bf16[128,2,128]{2,1,0:T(2,128)(2,1)} async-done(((bf16[128,2,128]{2,1,0:T(2,128)(2,1)}), bf16[128,2,128]{2,1,0:T(2,128)(2,1)}, u32[]{:S(2)}, u32[]{:S(2)}) %all-to-all-start.4) | async-done | bytes 65568 | tf_op jit(solution)/shard_map/all_to_all | solution.py:80
  113.3 6.9 %all-to-all-start.1 = ((bf16[128,2,128]{2,1,0:T(2,128)(2,1)}), bf16[128,2,128]{2,1,0:T(2,128)(2,1)}, u32[]{:S(2)}, u32[]{:S(2)}) async-start(bf16[128,2,128]{2,1,0:T(2,128)(2,1)} %bitcast.76), calls=%async_computation.1 | async-start | bytes 131072 | tf_op jit(solution)/shard_map/all_to_all | solution.py:81
  120.2 1.6 reshape.152
  121.8 1.9 fusion.6
  123.7 1.2 fusion.50
  124.9 6.7 %all-to-all-done.1 = bf16[128,2,128]{2,1,0:T(2,128)(2,1)} async-done(((bf16[128,2,128]{2,1,0:T(2,128)(2,1)}), bf16[128,2,128]{2,1,0:T(2,128)(2,1)}, u32[]{:S(2)}, u32[]{:S(2)}) %all-to-all-start.1) | async-done | bytes 65568 | tf_op jit(solution)/shard_map/all_to_all | solution.py:81
  132.6 2.1 fusion.7
  136.4 7.4 %all-to-all-start.5 = ((bf16[128,2,128]{2,1,0:T(2,128)(2,1)}), bf16[128,2,128]{2,1,0:T(2,128)(2,1)S(1)}, u32[]{:S(2)}, u32[]{:S(2)}) async-start(bf16[128,2,128]{2,1,0:T(2,128)(2,1)} %convert_element_type.92), calls=%async_computation.5 | async-start | bytes 131072 | tf_op jit(solution)/shard_map/all_to_all | solution.py:91
  143.8 2.7 fusion.18
  146.5 1.1 copy.69
  147.6 7.6 %all-to-all-done.5 = bf16[128,2,128]{2,1,0:T(2,128)(2,1)S(1)} async-done(((bf16[128,2,128]{2,1,0:T(2,128)(2,1)}), bf16[128,2,128]{2,1,0:T(2,128)(2,1)S(1)}, u32[]{:S(2)}, u32[]{:S(2)}) %all-to-all-start.5) | async-done | bytes 65568 | tf_op jit(solution)/shard_map/all_to_all | solution.py:91
  155.2 2.0 scatter_custom_fusion
  157.2 2.2 fusion.28
  159.4 3.3 %convolution_add_fusion = f32[512,512]{1,0:T(8,128)} fusion(f32[512,512]{1,0:T(8,128)} %fusion.28, bf16[512,512]{1,0:T(8,128)(2,1)} %param.24, bf16[512,512]{1,0:T(8,128)(2,1)S(1)} %fusion.11, bf16[512,512]{1,0:T(8,128)(2,1)} %param.23, f32[512,512]{1,0:T(8,128)S(1)} %fusion.55), kind=kOutput, calls=%fused_computation.12 | convolution fusion | flops 538705920 | bytes 4718592 | tf_op jit(solution)/shard_map/dot_general | solution.py:111
  165.3 18.2 %reduce-scatter.2.cloned.1.call-done = f32[128,512]{1,0:T(8,128)} async-done(((f32[512,512]{1,0:T(8,128)}), f32[128,512]{1,0:T(8,128)}) %reduce-scatter.2.cloned.1.call-update) | async-done | bytes 262160 | tf_op jit(solution)/shard_map/reduce_scatter | solution.py:110
  184.9 98.6 %psum.7 = f32[16,512]{1,0:T(8,128)S(1)} all-reduce(f32[16,512]{1,0:T(8,128)S(1)} %fusion.38), channel_id=1, replica_groups=mesh['round'=128,'mp'=4] {'round','mp'}, use_global_device_ids=true, to_apply=%region_8.9 | all-reduce | flops 8192 | bytes 65536 | tf_op jit(solution)/shard_map/psum | solution.py:126
  (60 shorter events, 17.2 us)
Async XLA Ops:
  7.2 20.7 %copy-start = (bf16[1,512,512]{2,1,0:T(8,128)(2,1)S(1)}, bf16[1,512,512]{2,1,0:T(8,128)(2,1)}, u32[]{:S(2)}) copy-start(bf16[1,512,512]{2,1,0:T(8,128)(2,1)} %param.13) | copy-start | bytes 1572868
  8.7 29.8 %all-to-all-start.2 = ((bf16[128,1,2]{2,1,0:T(2,128)(2,1)}), bf16[128,1,2]{2,1,0:T(2,128)(2,1)S(1)}, u32[]{:S(2)}, u32[]{:S(2)}) async-start(bf16[128,1,2]{2,1,0:T(2,128)(2,1)} %copy.61), calls=%async_computation.2 | async-start | bytes 131072 | tf_op jit(solution)/shard_map/all_to_all | solution.py:82
  35.0 14.9 %copy-start.6 = (s32[1,128,2]{1,2,0:T(2,128)S(1)}, s32[1,128,2]{1,2,0:T(2,128)}, u32[]{:S(2)}) copy-start(s32[1,128,2]{1,2,0:T(2,128)} %param.15) | copy-start | bytes 3076
  38.5 31.9 %all-to-all-start = ((bf16[128,2,1024]{2,1,0:T(2,128)(2,1)}), bf16[128,2,1024]{2,1,0:T(2,128)(2,1)S(1)}, u32[]{:S(2)}, u32[]{:S(2)}) async-start(bf16[128,2,1024]{2,1,0:T(2,128)(2,1)} %reshape.218), calls=%async_computation | async-start | bytes 1048576 | tf_op jit(solution)/shard_map/all_to_all | solution.py:59
  71.9 0.7 copy-start.7
  72.1 0.9 copy-start.3
  72.6 0.9 copy-start.4
  77.0 17.0 %all-to-all-start.3 = ((bf16[128,2,128]{2,1,0:T(2,128)(2,1)}), bf16[128,2,128]{2,1,0:T(2,128)(2,1)}, u32[]{:S(2)}, u32[]{:S(2)}) async-start(bf16[128,2,128]{2,1,0:T(2,128)(2,1)} %bitcast.12), calls=%async_computation.3 | async-start | bytes 131072 | tf_op jit(solution)/shard_map/all_to_all | solution.py:79
  83.3 1.5 copy-start.5
  94.1 19.2 %all-to-all-start.4 = ((bf16[128,2,128]{2,1,0:T(2,128)(2,1)}), bf16[128,2,128]{2,1,0:T(2,128)(2,1)}, u32[]{:S(2)}, u32[]{:S(2)}) async-start(bf16[128,2,128]{2,1,0:T(2,128)(2,1)} %bitcast.78), calls=%async_computation.4 | async-start | bytes 131072 | tf_op jit(solution)/shard_map/all_to_all | solution.py:80
  113.3 18.3 %all-to-all-start.1 = ((bf16[128,2,128]{2,1,0:T(2,128)(2,1)}), bf16[128,2,128]{2,1,0:T(2,128)(2,1)}, u32[]{:S(2)}, u32[]{:S(2)}) async-start(bf16[128,2,128]{2,1,0:T(2,128)(2,1)} %bitcast.76), calls=%async_computation.1 | async-start | bytes 131072 | tf_op jit(solution)/shard_map/all_to_all | solution.py:81
  136.4 18.8 %all-to-all-start.5 = ((bf16[128,2,128]{2,1,0:T(2,128)(2,1)}), bf16[128,2,128]{2,1,0:T(2,128)(2,1)S(1)}, u32[]{:S(2)}, u32[]{:S(2)}) async-start(bf16[128,2,128]{2,1,0:T(2,128)(2,1)} %convert_element_type.92), calls=%async_computation.5 | async-start | bytes 131072 | tf_op jit(solution)/shard_map/all_to_all | solution.py:91
  143.8 39.8 %reduce-scatter.2.cloned.1.call-start = ((), (), s32[]{:S(2)}) async-start(), calls=%async_computation.7 | async-start | bytes 1310720 | tf_op jit(solution)/shard_map/reduce_scatter | solution.py:110
  162.7 0.8 copy-start.2
  163.5 120.0 %copy-start.8 = (f32[512]{0:T(512)S(1)}, f32[512]{0:T(512)}, u32[]{:S(2)}) copy-start(f32[512]{0:T(512)} %param.25) | copy-start | bytes 6148
  184.6 99.6 %copy-start.1 = (bf16[32,4,512]{2,1,0:T(4,128)(2,1)}, bf16[32,4,512]{2,1,0:T(4,128)(2,1)S(1)}, u32[]{:S(2)}) copy-start(bf16[32,4,512]{2,1,0:T(4,128)(2,1)S(1)} %reshape.153) | copy-start | bytes 393220
Sparse Core Ops, SparseCore 0:
  162.9 20.6 reduce-scatter.1
where the time goes:
time: 292 us; the launch traced here: 291 us
  blocking collectives  98.6 us (34%)
  waiting for transfers between devices  68.8 us (24%)
  starting transfers between devices  58.4 us (20%)
  local copies, waits for them, and re-layouts  20.8 us (7%)
  matrix products  19.2 us (7%)
  between operations  14.4 us (5%)
  other arithmetic  10.9 us (4%)
    psum x1, blocking collectives, shards(): pooled = lax.psum(partial_sum, ('round', 'mp'))  98.6 us
    all_to_all x1, waiting for transfers between devices, shards(): lax.all_to_all(permuted, 'round', split_axis=1, concat_axis=0, tiled=True)  19.6 us
    all_to_all x1, starting transfers between devices, shards(): lax.all_to_all(live_slot.astype(jnp.bfloat16), 'round', split_axis=0, con...  18.4 us
    reduce_scatter x1, waiting for transfers between devices, shards(): lax.psum_scatter(attn_part + jnp.dot(hidden, w_down, preferred_element_ty...  18.2 us
    all_to_all x1, starting transfers between devices, shards(): lax.all_to_all(permuted, 'round', split_axis=1, concat_axis=0, tiled=True)  11.3 us
    all_to_all x1, waiting for transfers between devices, shards(): lax.all_to_all(keys_all[safe_rows], 'round', split_axis=0, concat_axis=0,...  8.46 us
    all_to_all x1, starting transfers between devices, shards(): lax.all_to_all(keys_all[safe_rows], 'round', split_axis=0, concat_axis=0,...  8.03 us
    all_to_all x1, waiting for transfers between devices, shards(): lax.all_to_all(seam_attn.reshape(round_count, -1, head_width), 'round', s...  7.59 us
  transfers between devices with their start and end apart: 7, of which 7 were waited for; matrix products, arithmetic and copies ran while one was open for 10% of the time, Pallas kernels for 0%

commit v1 on v0

v1 whole, which is shorter than its diff:
```python
import jax
import jax.numpy as jnp
from jax import lax
from jax.experimental import pallas as pl
from jax.experimental.pallas import tpu as pltpu
from jax.sharding import PartitionSpec as P

F32 = jnp.float32
BF16 = jnp.bfloat16
MESH = pl.DeviceIdType.MESH
EPS = 1e-6
NZ, NYK, NX = 8, 16, 4
D, HD, ROWS = 512, 128, 512
MARK = 2.0 ** 100
DEAD = -1e30


def iota(shape, axis):
    return lax.broadcasted_iota(jnp.int32, shape, axis)


def hot(mask):
    return jnp.where(mask, 1.0, 0.0).astype(BF16)


def mm(a, b):
    return jnp.dot(a, b, preferred_element_type=F32)


def mm_nt(a, b):
    return lax.dot_general(a, b, (((1,), (1,)), ((), ())), preferred_element_type=F32)


def softmax(scores):
    top = jnp.max(scores, axis=-1, keepdims=True)
    weights = jnp.exp((scores - top) * 0.125)
    total = jnp.sum(weights, axis=-1, keepdims=True)
    return (weights * (1.0 / total)).astype(BF16)


def kernel(
    tokens, cells, seam, obs, gain, w_q, w_k, w_v, w_o, w_g, w_u, w_d, w_r,
    out, logits,
    wqkv, wo, wg, wu, wd,
    x1, b1, x2, tok, normed, normed_c, qkv, q_c, local,
    sx1, sb1, sx2, sb2, ra, rb1, rx, rb2,
    hot_t, ff, ffb, cx, cb, px, pz, py,
    w_sem, wo_send, wo_recv, s_send, s_recv, y_send, y_recv, x_send, x_recv,
    f_send, f_recv,
):
    me = lax.axis_index("round")
    m = lax.axis_index("mp")
    z = me // NYK
    yk = lax.rem(me, NYK)

    def at_z(i):
        return (i * NYK + yk, m)

    def at_yk(i):
        return (z * NYK + i, m)

    def at_x(i):
        return (me, i)

    def peer(kind, k):
        if kind == "z":
            i = lax.rem(z + k, NZ)
            return i, at_z(i)
        if kind == "y":
            i = lax.rem(yk + k, NYK)
            return i, at_yk(i)
        i = lax.rem(m + k, NX)
        return i, at_x(i)

    counts = {"z": NZ, "y": NYK, "x": NX}

    barrier = pltpu.get_barrier_semaphore()
    for kind in ("z", "y", "x"):
        for k in range(1, counts[kind]):
            pl.semaphore_signal(
                barrier, inc=1, device_id=peer(kind, k)[1], device_id_type=MESH
            )

    loads = [
        pltpu.make_async_copy(w_q, wqkv.at[:, pl.ds(0, HD)], w_sem.at[0]),
        pltpu.make_async_copy(w_k, wqkv.at[:, pl.ds(HD, HD)], w_sem.at[1]),
        pltpu.make_async_copy(w_v, wqkv.at[:, pl.ds(2 * HD, HD)], w_sem.at[2]),
        pltpu.make_async_copy(w_g, wg, w_sem.at[3]),
        pltpu.make_async_copy(w_u, wu, w_sem.at[4]),
        pltpu.make_async_copy(w_d, wd, w_sem.at[5]),
        pltpu.make_async_copy(w_o, wo.at[m], w_sem.at[6]),
    ]
    for load in loads:
        load.start()

    def exchange(kind, src, dst, send, recv):
        started = []
        for k in range(1, counts[kind]):
            i, where = peer(kind, k)
            copy = pltpu.make_async_remote_copy(
                src_ref=src(i),
                dst_ref=dst,
                send_sem=send.at[k],
                recv_sem=recv.at[k],
                device_id=where,
                device_id_type=MESH,
            )
            copy.start()
            started.append(copy)
        return started

    def finish(started):
        for copy in started:
            copy.wait()

    cell_row = cells[...].astype(F32)
    pick = iota((128, 512), 1) == 4 * iota((128, 512), 0) + m
    cell_col = jnp.sum(jnp.where(pick, cell_row, 0.0), axis=1, keepdims=True)
    lanes_f = iota((128, 512), 1).astype(F32)
    x1[...] = mm(hot(lanes_f == cell_col), tokens[...]).astype(BF16).reshape(NZ, NYK, D)

    pl.semaphore_wait(barrier, (NZ - 1) + (NYK - 1) + (NX - 1))
    stage_z = exchange("z", lambda i: x1.at[i], b1.at[z], s_send.at[0], s_recv.at[0])
    loads[6].wait()
    share_wo = exchange("x", lambda i: wo.at[m], wo.at[m], wo_send, wo_recv)
    b1[z] = x1[z]

    own_pick = iota((128, 512), 1) == 4 * me + (iota((128, 512), 0) & 3)
    own_col = jnp.sum(jnp.where(own_pick, cell_row, 0.0), axis=1, keepdims=True)
    obs_all = jnp.concatenate(
        [obs[...].astype(F32), jnp.zeros((112, 512), F32)], axis=0
    ).astype(BF16)
    support = mm_nt(hot(lanes_f == own_col), obs_all)
    divisor = jnp.sqrt(128.0 * mm_nt(jnp.ones((8, 512), BF16), obs_all))[0:1]

    rows = seam[...]
    shuffled = (rows & 3) * 128 + ((rows >> 2) & 15) * 8 + (rows >> 6)
    shuffled = jnp.where(rows < 0, -1, shuffled)
    hot_g = jnp.concatenate(
        [hot(iota((128, 512), 1) == shuffled[:, c : c + 1]) for c in range(2)], axis=0
    )
    hot_c = jnp.concatenate(
        [hot(iota((128, 512), 1) == rows[:, c : c + 1]) for c in range(2)], axis=0
    )
    empty = jnp.concatenate([rows[:, c : c + 1] < 0 for c in range(2)], axis=0)
    hot_t[...] = hot_c.astype(F32).T.astype(BF16)

    q, p = iota((128, 128), 0), iota((128, 128), 1)
    turn = hot(p == (q & 7) * NYK + (q >> 3))
    finish(stage_z)
    x2[...] = mm(turn, b1[...].reshape(128, D)).astype(BF16).reshape(NYK, NZ, D)
    mine = tok.at[m]
    stage_y = exchange("y", lambda i: x2.at[i], mine.at[yk], y_send.at[0], y_recv.at[0])
    tok[m, yk] = x2[yk]
    for load in loads[:3]:
        load.wait()
    finish(stage_y)

    stage_x = exchange("x", lambda i: tok.at[m], tok.at[m], x_send.at[0], x_recv.at[0])
    gain_row = gain[...]
    finish(stage_x)

    def norm_step(c, carry):
        values = tok[c].reshape(128, D).astype(F32)
        spread = jnp.mean(values * values, axis=-1, keepdims=True)
        normal = (values * lax.rsqrt(spread + EPS) * gain_row).astype(BF16)
        at = pl.ds(pl.multiple_of(c * 128, 128), 128)
        normed[at, :] = normal
        qkv[at, :] = mm(normal, wqkv[...]).astype(BF16)
        return carry

    lax.fori_loop(0, 4, norm_step, 0)

    sent = mm(hot_g, qkv[...])
    lane = iota((256, 384), 1)
    sent = jnp.where((lane == 0) & empty, MARK, sent).astype(BF16)
    sx1[...] = sent.reshape(2, NZ, NYK, 3 * HD)
    seam_z = exchange("z", lambda i: sx1.at[:, i], sb1.at[z], s_send.at[1], s_recv.at[1])
    sb1[z] = sx1[:, z]

    a, b = iota((512, 512), 0), iota((512, 512), 1)
    natural = hot(b == (a & 3) * 128 + ((a >> 2) & 15) * 8 + (a >> 6))
    normed_c[...] = mm(natural, normed[...]).astype(BF16)
    q_c[...] = mm(natural, qkv[:, 0:HD]).astype(BF16)
    loads[3].wait()
    loads[4].wait()
    loads[5].wait()

    def ff_step(i, carry):
        at = pl.ds(pl.multiple_of(i * 128, 128), 128)
        block = normed_c[at, :]
        gate = mm(block, wg[...])
        up = mm(block, wu[...])
        hidden = (gate * (1.0 / (1.0 + jnp.exp(-gate))) * up).astype(BF16)
        ff[i] = mm(hidden, wd[...])
        return carry

    lax.fori_loop(0, 4, ff_step, 0)
    share_ff = exchange("x", lambda i: ff.at[i], ffb.at[m], f_send, f_recv)

    q2, p2 = iota((256, 256), 0), iota((256, 256), 1)
    turn_out = hot(p2 == (q2 & 7) * 32 + ((q2 >> 3) & 1) * 16 + (q2 >> 4))
    finish(seam_z)
    sx2[...] = mm(turn_out, sb1[...].reshape(256, 3 * HD)).astype(BF16).reshape(NYK, 16, 3 * HD)
    seam_y = exchange("y", lambda i: sx2.at[i], sb2.at[yk], y_send.at[1], y_recv.at[1])
    sb2[yk] = sx2[yk]
    ffb[m] = ff[m]

    low = iota((512, HD), 1) < 64
    for h in range(2):
        half = low if h == 0 else jnp.logical_not(low)
        keys = jnp.where(half, qkv[:, HD : 2 * HD], 0.0).astype(BF16)
        values = jnp.where(half, qkv[:, 2 * HD : 3 * HD], 0.0).astype(BF16)
        for blk in range(2):
            at = slice(blk * 256, blk * 256 + 256)
            weights = softmax(mm_nt(q_c[at, :], keys))
            mix = mm(weights, values)
            if h == 0:
                local[at, :] = mix
            else:
                local[at, :] += mix

    finish(seam_y)
    held = sb2[...].reshape(256, 3 * HD)
    sq, sk, sv = held[:, 0:HD], held[:, HD : 2 * HD], held[:, 2 * HD :]
    dead = sq[:, 0:1].astype(F32) > 1e20
    lane2 = iota((256, HD), 1)
    low2 = lane2 < 64
    total = jnp.zeros((256, HD), F32)
    sq = jnp.where(dead, 0.0, sq.astype(F32))
    skf, svf = sk.astype(F32), sv.astype(F32)
    for h in range(2):
        half = low2 if h == 0 else jnp.logical_not(low2)
        spot = lane2 == (64 if h == 0 else 0)
        queries = jnp.where(half, sq, jnp.where(spot, 1.0, 0.0)).astype(BF16)
        keys = jnp.where(half, skf, jnp.where(spot & dead, DEAD, 0.0)).astype(BF16)
        values = jnp.where(half, svf, 0.0).astype(BF16)
        total += mm(softmax(mm_nt(queries, keys)), values)
    ra[...] = total.astype(BF16).reshape(NYK, 16, HD)
    back_y = exchange("y", lambda i: ra.at[i], rb1.at[yk], y_send.at[2], y_recv.at[2])
    rb1[yk] = ra[yk]

    a2, b2 = iota((128, 512), 0) + 128 * m, iota((128, 512), 1)
    own = hot(b2 == (a2 & 3) * 128 + ((a2 >> 2) & 15) * 8 + (a2 >> 6))
    own_tok = mm(own, tok[...].reshape(ROWS, D))

    turn_back = hot(p2 == (q2 & 15) * 16 + ((q2 >> 4) & 1) * 8 + (q2 >> 5))
    finish(back_y)
    rx[...] = mm(turn_back, rb1[...].reshape(256, HD)).astype(BF16).reshape(NZ, 2, NYK, HD)
    back_z = exchange("z", lambda i: rx.at[i], rb2.at[:, z], s_send.at[2], s_recv.at[2])
    rb2[:, z] = rx[z]
    finish(share_wo)
    finish(share_ff)
    ff_own = ffb[0] + ffb[1] + ffb[2] + ffb[3]
    finish(back_z)

    both = local[...] + mm(hot_t[...], rb2[...].reshape(256, HD))
    cx[...] = both.astype(BF16).reshape(NX, 128, HD)
    comb_x = exchange("x", lambda i: cx.at[i], cb.at[m], x_send.at[1], x_recv.at[1])
    cb[m] = cx[m]
    finish(comb_x)
    attn = mm(cb[0], wo[0]) + mm(cb[1], wo[1]) + mm(cb[2], wo[2]) + mm(cb[3], wo[3])
    result = (own_tok + (attn + ff_own)).astype(BF16)
    out[...] = result

    dots = jnp.sum(result.astype(F32) * w_r[...], axis=1, keepdims=True)
    px[m] = jnp.sum(support * dots, axis=0, keepdims=True)
    sum_x = exchange("x", lambda i: px.at[m], px.at[m], x_send.at[2], x_recv.at[2])
    finish(sum_x)
    pz[z] = jnp.sum(px[...], axis=0)
    sum_z = exchange("z", lambda i: pz.at[z], pz.at[z], s_send.at[3], s_recv.at[3])
    finish(sum_z)
    py[yk] = jnp.sum(pz[...], axis=0)
    sum_y = exchange("y", lambda i: py.at[yk], py.at[yk], y_send.at[3], y_recv.at[3])
    finish(sum_y)
    pooled = jnp.sum(py[...], axis=0)
    logits[...] = (pooled / divisor)[:, 0:16]


def shards(
    tokens, cell_order, seam_rows, obs_mask, norm_gain,
    w_query, w_key, w_value, w_out, w_gate, w_up, w_down, w_read,
):
    vmem = pl.BlockSpec(memory_space=pltpu.VMEM)
    hbm = pl.BlockSpec(memory_space=pl.ANY)
    dma = pltpu.SemaphoreType.DMA
    V = pltpu.VMEM
    out, logits = pl.pallas_call(
        kernel,
        out_shape=(
            jax.ShapeDtypeStruct((128, D), BF16),
            jax.ShapeDtypeStruct((1, 16), F32),
        ),
        in_specs=[vmem] * 5 + [hbm] * 7 + [vmem],
        out_specs=(vmem, vmem),
        scratch_shapes=[
            V((D, 3 * HD), BF16), V((NX, HD, D), BF16), V((D, D), BF16),
            V((D, D), BF16), V((D, D), BF16),
            V((NZ, NYK, D), BF16), V((NZ, NYK, D), BF16), V((NYK, NZ, D), BF16),
            V((NX, NYK, NZ, D), BF16), V((ROWS, D), BF16), V((ROWS, D), BF16),
            V((ROWS, 3 * HD), BF16), V((ROWS, HD), BF16), V((ROWS, HD), F32),
            V((2, NZ, NYK, 3 * HD), BF16), V((NZ, 2, NYK, 3 * HD), BF16),
            V((NYK, 16, 3 * HD), BF16), V((NYK, 16, 3 * HD), BF16),
            V((NYK, 16, HD), BF16), V((NYK, 16, HD), BF16),
            V((NZ, 2, NYK, HD), BF16), V((2, NZ, NYK, HD), BF16),
            V((ROWS, 256), BF16), V((NX, 128, D), F32), V((NX, 128, D), F32),
            V((NX, 128, HD), BF16), V((NX, 128, HD), BF16),
            V((NX, 1, 128), F32), V((NZ, 1, 128), F32), V((NYK, 1, 128), F32),
            dma((7,)), dma((NX,)), dma((NX,)),
            dma((4, NZ)), dma((4, NZ)), dma((4, NYK)), dma((4, NYK)),
            dma((3, NX)), dma((3, NX)), dma((NX,)), dma((NX,)),
        ],
        compiler_params=pltpu.CompilerParams(
            collective_id=0, has_side_effects=True, vmem_limit_bytes=40 * 2 ** 20
        ),
    )(
        tokens.reshape(512, D), cell_order.reshape(1, 512), seam_rows.reshape(128, 2),
        obs_mask, norm_gain.reshape(1, D), w_query, w_key, w_value, w_out, w_gate,
        w_up, w_down, w_read.reshape(1, D),
    )
    return out.reshape(32, 4, D), logits.reshape(16)


def solution(mesh):
    return jax.shard_map(
        shards,
        mesh=mesh,
        in_specs=(
            P("round", None, None),
            P(),
            P("round", None, None),
            P(),
            P(),
            P(None, "mp"),
            P(None, "mp"),
            P(None, "mp"),
            P("mp", None),
            P(None, "mp"),
            P(None, "mp"),
            P("mp", None),
            P(),
        ),
        out_specs=(P("mp", "round", None), P()),
        check_vma=False,
    )
```

time: 292 us -> 91.9 us (0.31)
  blocking collectives: 98.6 us -> 0 us
  Pallas kernels: 0 us -> 80.3 us
  waiting for transfers between devices: 68.8 us -> 0 us
  starting transfers between devices: 58.4 us -> 0 us
  matrix products: 19.2 us -> 0 us
  between operations: 14.4 us -> 0.67 us
  other arithmetic: 10.9 us -> 0 us
  local copies, waits for them, and re-layouts: 20.8 us -> 10.4 us
    psum x1 -> x0, blocking collectives: 98.6 us -> none  [shards(): pooled = lax.psum(partial_sum, ('round', 'mp'))]
    pallas_call x0 -> x1, Pallas kernels: none -> 80.3 us  [shards(): pl.pallas_call(kernel, out_shape=(jax.ShapeDtypeStruct((128, D), BF16), j...]
    all_to_all x6 -> x0, starting transfers between devices: 58.3 us -> none  [the longest x1 18.4 us: shards(): lax.all_to_all(live_slot.astype(jnp.bfloat16), 'round', split_axis=0, con...]
    all_to_all x6 -> x0, waiting for transfers between devices: 50.6 us -> none  [the longest x1 19.6 us: shards(): lax.all_to_all(permuted, 'round', split_axis=1, concat_axis=0, tiled=True)]
    reduce_scatter x1 -> x0, waiting for transfers between devices: 18.2 us -> none  [shards(): lax.psum_scatter(attn_part + jnp.dot(hidden, w_down, preferred_element_ty...]
    dot_general x11 -> x0, matrix products: 16.2 us -> none  [the longest x2 4.81 us: attend(): jnp.einsum('hqk,khe->qhe', probabilities, values_all, preferred_element_t...]
    gather x6 -> x0, local copies, waits for them, and re-layouts: 7.72 us -> none  [the longest x2 2.78 us: shards(): permuted = tokens[:, cell_order, :]]
    unnamed x23 -> x28, local copies, waits for them, and re-layouts: 4.01 us -> 9.72 us
  transfers between devices with their start and end apart: 7 -> 0, of which waited for: 7 -> 0; matrix products, arithmetic and copies ran while one was open for 10% -> 0% of each run, Pallas kernels for 0% -> 0%
where the time goes in v1:
time: 91.9 us; the launch traced here: 91.4 us
  Pallas kernels  80.3 us (87%)
  local copies, waits for them, and re-layouts  10.4 us (11%)
    pallas_call x1, Pallas kernels, shards(): pl.pallas_call(kernel, out_shape=(jax.ShapeDtypeStruct((128, D), BF16), j...  80.3 us
    unnamed x28, local copies, waits for them, and re-layouts  9.72 us

profile of v1, /device:TPU:1, one launch (start us, length us, event | category | flops | bytes accessed | tf_op | source)
XLA Modules:
  0.0 91.4 jit_solution(15069519992080181727)
XLA Ops:
  0.6 0.0 copy-start.12
  0.6 0.7 copy-done.12
  1.3 0.0 copy-start.8
  1.3 0.0 copy-start.9
  1.3 0.0 copy-start.10
  1.3 0.0 copy-start.11
  1.3 0.1 copy.15
  1.4 0.6 copy-done.8
  2.1 0.0 copy-done.9
  2.1 0.0 copy-done.10
  2.1 0.0 copy-done.11
  2.1 0.0 copy-start
  2.1 1.0 %copy-done = bf16[1,512,512]{2,1,0:T(8,128)(2,1)S(1)} copy-done((bf16[1,512,512]{2,1,0:T(8,128)(2,1)S(1)}, bf16[1,512,512]{2,1,0:T(8,128)(2,1)}, u32[]{:S(2)}) %copy-start) | copy-done | bytes 524312
  3.1 0.0 copy-start.1
  3.1 1.0 %copy-done.1 = bf16[512,512]{1,0:T(8,128)(2,1)S(1)} copy-done((bf16[512,512]{1,0:T(8,128)(2,1)S(1)}, bf16[512,512]{1,0:T(8,128)(2,1)}, u32[]{:S(2)}) %copy-start.1) | copy-done | bytes 524312
  4.2 0.0 copy-start.2
  4.2 1.0 %copy-done.2 = bf16[512,512]{1,0:T(8,128)(2,1)S(1)} copy-done((bf16[512,512]{1,0:T(8,128)(2,1)S(1)}, bf16[512,512]{1,0:T(8,128)(2,1)}, u32[]{:S(2)}) %copy-start.2) | copy-done | bytes 524312
  5.2 0.0 copy-start.3
  5.2 1.0 %copy-done.3 = bf16[512,512]{1,0:T(8,128)(2,1)S(1)} copy-done((bf16[512,512]{1,0:T(8,128)(2,1)S(1)}, bf16[512,512]{1,0:T(8,128)(2,1)}, u32[]{:S(2)}) %copy-start.3) | copy-done | bytes 524312
  6.2 0.0 copy-start.4
  6.2 0.9 copy-done.4
  7.2 0.0 copy-start.5
  7.2 0.9 copy-done.5
  8.1 0.0 copy-start.6
  8.1 0.9 copy-done.6
  9.0 0.0 copy-start.7
  9.0 0.9 copy-done.7
  9.9 80.3 %shard_map.140 = (bf16[128,512]{1,0:T(8,128)(2,1)S(1)}, f32[1,16]{1,0:T(1,128)S(1)}) custom-call(bf16[512,512]{1,0:T(8,128)(2,1)S(1)} %bitcast.6, s32[1,512]{1,0:T(1,128)S(1)} %bitcast.8, s32[128,2]{1,0:T(8,128)S(1)} %bitcast.7, s32[16,512]{1,0:T(8,128)S(1)} %copy-done.8, f32[1,512]{1,0:T(1,128)S(1)} %bitcast.9, bf16[512,128]{1,0:T(8,128)(2,1)S(1)} %copy-done.4, ...), custom_call_target="tpu_custom_call" | custom-call | tf_op jit(solution)/shard_map/pallas_call | solution.py:288
  90.2 0.7 reshape.30
  90.9 0.5 copy.17
Async XLA Ops:
  0.6 0.7 copy-start.12
  1.3 0.8 copy-start.8
  1.3 0.8 copy-start.9
  1.3 0.8 copy-start.10
  1.3 0.8 copy-start.11
  2.1 1.0 %copy-start = (bf16[1,512,512]{2,1,0:T(8,128)(2,1)S(1)}, bf16[1,512,512]{2,1,0:T(8,128)(2,1)}, u32[]{:S(2)}) copy-start(bf16[1,512,512]{2,1,0:T(8,128)(2,1)} %param.13) | copy-start | bytes 1572868
  3.1 1.0 %copy-start.1 = (bf16[512,512]{1,0:T(8,128)(2,1)S(1)}, bf16[512,512]{1,0:T(8,128)(2,1)}, u32[]{:S(2)}) copy-start(bf16[512,512]{1,0:T(8,128)(2,1)} %w_g.1) | copy-start | bytes 1572868
  4.2 1.0 %copy-start.2 = (bf16[512,512]{1,0:T(8,128)(2,1)S(1)}, bf16[512,512]{1,0:T(8,128)(2,1)}, u32[]{:S(2)}) copy-start(bf16[512,512]{1,0:T(8,128)(2,1)} %w_u.1) | copy-start | bytes 1572868
  5.2 1.0 %copy-start.3 = (bf16[512,512]{1,0:T(8,128)(2,1)S(1)}, bf16[512,512]{1,0:T(8,128)(2,1)}, u32[]{:S(2)}) copy-start(bf16[512,512]{1,0:T(8,128)(2,1)} %w_d.1) | copy-start | bytes 1572868
  6.2 0.9 copy-start.4
  7.2 0.9 copy-start.5
  8.1 0.9 copy-start.6
  9.0 0.9 copy-start.7

commit v2 on v1

v2 whole, which is shorter than its diff:
```python
import jax
import jax.numpy as jnp
from jax import lax
from jax.experimental import pallas as pl
from jax.experimental.pallas import tpu as pltpu
from jax.sharding import PartitionSpec as P

F32 = jnp.float32
BF16 = jnp.bfloat16
MESH = pl.DeviceIdType.MESH
EPS = 1e-6
ROUNDS, NX = 128, 4
D, HD, ROWS, SLOTS = 512, 128, 512, 256
MARK = 2.0 ** 100
DEAD = -1e30


def iota(shape, axis):
    return lax.broadcasted_iota(jnp.int32, shape, axis)


def hot(mask):
    return jnp.where(mask, 1.0, 0.0).astype(BF16)


def mm(a, b):
    return jnp.dot(a, b, preferred_element_type=F32)


def mm_nt(a, b):
    return lax.dot_general(a, b, (((1,), (1,)), ((), ())), preferred_element_type=F32)


def softmax(scores):
    top = jnp.max(scores, axis=-1, keepdims=True)
    weights = jnp.exp((scores - top) * 0.125)
    total = jnp.sum(weights, axis=-1, keepdims=True)
    return (weights * (1.0 / total)).astype(BF16)


def kernel(
    tokens_hbm, cells, seam, obs, gain, w_q, w_k, w_v, w_o, w_g, w_u, w_d, w_r,
    out, logits,
    tokens, wqkv, wo, wg, wu, wd,
    x1, tok, normed, qkv, local, sx, sb, ra, rb, hot_t, ff, ffb, cx, cb, px, pr,
    w_sem, r_send, r_recv, x_send, x_recv,
):
    me = lax.axis_index("round")
    m = lax.axis_index("mp")
    z, y, core = me // 16, lax.rem(me // 2, 8), lax.rem(me, 2)

    def far_first(k):
        return 4 + (1 - 2 * lax.rem(k, 2)) * ((k + 1) // 2)

    def round_peer(k):
        to_z = lax.rem(z + far_first(k // 16), 8)
        to_y = lax.rem(y + far_first(lax.rem(k // 2, 8)), 8)
        to_core = lax.rem(core + 1 - lax.rem(k, 2), 2)
        return to_z * 16 + to_y * 2 + to_core

    def x_peer(k):
        return lax.rem(m + k, NX)

    def send_rounds(src, dst, slot):
        def step(k, carry):
            to = round_peer(k)
            pltpu.make_async_remote_copy(
                src_ref=src(to),
                dst_ref=dst.at[me],
                send_sem=r_send.at[slot],
                recv_sem=r_recv.at[slot],
                device_id=(to, m),
                device_id_type=MESH,
            ).start()
            return carry

        lax.fori_loop(0, ROUNDS - 1, step, 0)

    def wait_rounds(buffer, sem, slot):
        others = buffer.at[pl.ds(0, ROUNDS - 1)]
        pltpu.make_async_copy(others, others, sem.at[slot]).wait()

    def send_x(src, dst, slot):
        started = []
        for k in (2, 1, 3):
            to = x_peer(k)
            copy = pltpu.make_async_remote_copy(
                src_ref=src(to),
                dst_ref=dst,
                send_sem=x_send.at[slot, k],
                recv_sem=x_recv.at[slot, k],
                device_id=(me, to),
                device_id_type=MESH,
            )
            copy.start()
            started.append(copy)
        return started

    def finish(started):
        for copy in started:
            copy.wait()

    load_tokens = pltpu.make_async_copy(tokens_hbm, tokens, w_sem.at[7])
    load_tokens.start()
    barrier = pltpu.get_barrier_semaphore()

    def greet(k, carry):
        pl.semaphore_signal(
            barrier, inc=1, device_id=(round_peer(k), m), device_id_type=MESH
        )
        return carry

    lax.fori_loop(0, ROUNDS - 1, greet, 0)
    for k in range(1, NX):
        pl.semaphore_signal(
            barrier, inc=1, device_id=(me, x_peer(k)), device_id_type=MESH
        )

    loads = [
        pltpu.make_async_copy(w_q, wqkv.at[:, pl.ds(0, HD)], w_sem.at[0]),
        pltpu.make_async_copy(w_k, wqkv.at[:, pl.ds(HD, HD)], w_sem.at[1]),
        pltpu.make_async_copy(w_v, wqkv.at[:, pl.ds(2 * HD, HD)], w_sem.at[2]),
        pltpu.make_async_copy(w_g, wg, w_sem.at[3]),
        pltpu.make_async_copy(w_u, wu, w_sem.at[4]),
        pltpu.make_async_copy(w_d, wd, w_sem.at[5]),
        pltpu.make_async_copy(w_o, wo.at[m], w_sem.at[6]),
    ]
    for load in loads:
        load.start()

    cell_row = cells[...].astype(F32)
    diagonal = iota((128, 128), 0) == iota((128, 128), 1)
    lanes = iota((128, 512), 1)
    load_tokens.wait()
    for b in range(4):
        part = cell_row[:, b * 128 : b * 128 + 128]
        col = jnp.sum(jnp.where(diagonal, part, 0.0), axis=1, keepdims=True)
        picked = mm(hot(lanes == col.astype(jnp.int32)), tokens[...])
        x1[b * 32 : b * 32 + 32] = picked.astype(BF16).reshape(32, 4, D)
    pl.semaphore_wait(barrier, ROUNDS - 1 + NX - 1)
    send_rounds(lambda i: x1.at[i], tok, 0)
    tok[me] = x1[me]
    loads[6].wait()
    share_wo = send_x(lambda i: wo.at[m], wo.at[m], 0)

    own_pick = lanes == 4 * me + (iota((128, 512), 0) & 3)
    own_col = jnp.sum(jnp.where(own_pick, cell_row, 0.0), axis=1, keepdims=True)
    obs_all = jnp.concatenate(
        [obs[...].astype(F32), jnp.zeros((112, 512), F32)], axis=0
    ).astype(BF16)
    support = mm_nt(hot(lanes == own_col.astype(jnp.int32)), obs_all)
    divisor = jnp.sqrt(128.0 * mm_nt(jnp.ones((8, 512), BF16), obs_all))[0:1]

    s, o = iota((SLOTS, 128), 0), iota((SLOTS, 128), 1)
    both_rows = jnp.where((s & 1) == 0, seam[0:1], seam[1:2]).astype(F32)
    slot_col = jnp.sum(jnp.where(o == (s >> 1), both_rows, 0.0), axis=1, keepdims=True)
    empty = slot_col < 0.0
    hot_g = hot(iota((SLOTS, ROWS), 1) == slot_col.astype(jnp.int32))
    same = iota((SLOTS, SLOTS), 0) == iota((SLOTS, SLOTS), 1)
    slot_row = jnp.sum(jnp.where(same, slot_col, 0.0), axis=0, keepdims=True)
    hot_t[...] = hot(iota((ROWS, SLOTS), 0) == slot_row.astype(jnp.int32))

    gain_row = gain[...]
    for load in loads[:3]:
        load.wait()
    wait_rounds(tok, r_recv, 0)

    def norm_step(c, carry):
        values = tok[pl.ds(c * 32, 32)].reshape(128, D).astype(F32)
        spread = jnp.mean(values * values, axis=-1, keepdims=True)
        normal = (values * lax.rsqrt(spread + EPS) * gain_row).astype(BF16)
        at = pl.ds(pl.multiple_of(c * 128, 128), 128)
        normed[at, :] = normal
        qkv[at, :] = mm(normal, wqkv[...]).astype(BF16)
        return carry

    lax.fori_loop(0, 4, norm_step, 0)

    sent = mm(hot_g, qkv[...])
    sent = jnp.where((iota((SLOTS, 3 * HD), 1) == 0) & empty, MARK, sent).astype(BF16)
    sx[...] = sent.reshape(ROUNDS, 2, 3 * HD)
    send_rounds(lambda i: sx.at[i], sb, 1)
    sb[me] = sx[me]

    for load in loads[3:6]:
        load.wait()

    def ff_step(i, carry):
        block = normed[pl.ds(pl.multiple_of(i * 128, 128), 128), :]
        gate = mm(block, wg[...])
        up = mm(block, wu[...])
        hidden = (gate * (1.0 / (1.0 + jnp.exp(-gate))) * up).astype(BF16)
        ff[i] = mm(hidden, wd[...])
        return carry

    lax.fori_loop(0, 4, ff_step, 0)
    share_ff = send_x(lambda i: ff.at[i], ffb.at[m], 1)
    ffb[m] = ff[m]

    low = iota((ROWS, HD), 1) < 64
    for h in range(2):
        half = low if h == 0 else jnp.logical_not(low)
        keys = jnp.where(half, qkv[:, HD : 2 * HD], 0.0).astype(BF16)
        values = jnp.where(half, qkv[:, 2 * HD : 3 * HD], 0.0).astype(BF16)
        for blk in range(2):
            at = slice(blk * 256, blk * 256 + 256)
            mix = mm(softmax(mm_nt(qkv[at, 0:HD], keys)), values)
            if h == 0:
                local[at, :] = mix
            else:
                local[at, :] += mix

    wait_rounds(sb, r_recv, 1)
    held = sb[...].reshape(SLOTS, 3 * HD)
    sq = held[:, 0:HD].astype(F32)
    sk, sv = held[:, HD : 2 * HD].astype(F32), held[:, 2 * HD :].astype(F32)
    dead = sq[:, 0:1] > 1e20
    sq = jnp.where(dead, 0.0, sq)
    lane = iota((SLOTS, HD), 1)
    total = jnp.zeros((SLOTS, HD), F32)
    for h in range(2):
        half = lane < 64 if h == 0 else lane >= 64
        spot = lane == (64 if h == 0 else 0)
        queries = jnp.where(half, sq, jnp.where(spot, 1.0, 0.0)).astype(BF16)
        keys = jnp.where(half, sk, jnp.where(spot & dead, DEAD, 0.0)).astype(BF16)
        values = jnp.where(half, sv, 0.0).astype(BF16)
        total += mm(softmax(mm_nt(queries, keys)), values)
    ra[...] = total.astype(BF16).reshape(ROUNDS, 2, HD)
    send_rounds(lambda i: ra.at[i], rb, 2)
    rb[me] = ra[me]

    own_tok = tok[pl.ds(m * 32, 32)].reshape(128, D).astype(F32)
    finish(share_wo)
    finish(share_ff)
    ff_own = ffb[0] + ffb[1] + ffb[2] + ffb[3]
    wait_rounds(rb, r_recv, 2)

    both = local[...] + mm(hot_t[...], rb[...].reshape(SLOTS, HD))
    cx[...] = both.astype(BF16).reshape(NX, 128, HD)
    comb_x = send_x(lambda i: cx.at[i], cb.at[m], 2)
    cb[m] = cx[m]
    finish(comb_x)
    attn = mm(cb[0], wo[0]) + mm(cb[1], wo[1]) + mm(cb[2], wo[2]) + mm(cb[3], wo[3])
    result = (own_tok + (attn + ff_own)).astype(BF16)
    out[...] = result.reshape(32, 4, D)

    dots = jnp.sum(result.astype(F32) * w_r[...], axis=1, keepdims=True)
    px[m] = jnp.sum(support * dots, axis=0, keepdims=True)
    sum_x = send_x(lambda i: px.at[m], px.at[m], 3)
    finish(sum_x)
    pr[me] = jnp.sum(px[...], axis=0)
    send_rounds(lambda i: pr.at[me], pr, 3)
    wait_rounds(pr, r_recv, 3)
    pooled = jnp.sum(pr[...], axis=0)
    logits[...] = (pooled / divisor)[:, 0:16]
    for slot, buffer in enumerate((tok, sb, rb, pr)):
        wait_rounds(buffer, r_send, slot)


def in_hbm(array):
    return pltpu.with_memory_space_constraint(array, pltpu.HBM)


def shards(
    tokens, cell_order, seam_rows, obs_mask, norm_gain,
    w_query, w_key, w_value, w_out, w_gate, w_up, w_down, w_read,
):
    vmem = pl.BlockSpec(memory_space=pltpu.VMEM)
    hbm = pl.BlockSpec(memory_space=pltpu.HBM)
    dma = pltpu.SemaphoreType.DMA
    V = pltpu.VMEM
    out, logits = pl.pallas_call(
        kernel,
        out_shape=(
            jax.ShapeDtypeStruct((32, 4, D), BF16),
            jax.ShapeDtypeStruct((1, 16), F32),
        ),
        in_specs=[hbm] + [vmem] * 4 + [hbm] * 7 + [vmem],
        out_specs=(vmem, vmem),
        scratch_shapes=[
            V((D, D), BF16), V((D, 3 * HD), BF16), V((NX, HD, D), BF16),
            V((D, D), BF16), V((D, D), BF16), V((D, D), BF16),
            V((ROUNDS, 4, D), BF16), V((ROUNDS, 4, D), BF16), V((ROWS, D), BF16),
            V((ROWS, 3 * HD), BF16), V((ROWS, HD), F32),
            V((ROUNDS, 2, 3 * HD), BF16), V((ROUNDS, 2, 3 * HD), BF16),
            V((ROUNDS, 2, HD), BF16), V((ROUNDS, 2, HD), BF16),
            V((ROWS, SLOTS), BF16), V((NX, 128, D), F32), V((NX, 128, D), F32),
            V((NX, 128, HD), BF16), V((NX, 128, HD), BF16),
            V((NX, 1, 128), F32), V((ROUNDS, 1, 128), F32),
            dma((8,)), dma((4,)), dma((4,)), dma((4, NX)), dma((4, NX)),
        ],
        compiler_params=pltpu.CompilerParams(
            collective_id=0, has_side_effects=True, vmem_limit_bytes=40 * 2 ** 20
        ),
    )(
        in_hbm(tokens.reshape(512, D)), cell_order.reshape(1, 512), seam_rows[0].T,
        obs_mask, norm_gain.reshape(1, D),
        *[in_hbm(w) for w in (w_query, w_key, w_value, w_out, w_gate, w_up, w_down)],
        w_read.reshape(1, D),
    )
    return out, logits.reshape(16)


def solution(mesh):
    return jax.shard_map(
        shards,
        mesh=mesh,
        in_specs=(
            P("round", None, None),
            P(),
            P("round", None, None),
            P(),
            P(),
            P(None, "mp"),
            P(None, "mp"),
            P(None, "mp"),
            P("mp", None),
            P(None, "mp"),
            P(None, "mp"),
            P("mp", None),
            P(),
        ),
        out_specs=(P("mp", "round", None), P()),
        check_vma=False,
    )
```

time: 91.9 us -> 85.4 us (0.929)
  local copies, waits for them, and re-layouts: 10.4 us -> 2.62 us
  Pallas kernels: 80.3 us -> 81.8 us
    unnamed x28 -> x12, local copies, waits for them, and re-layouts: 9.72 us -> 2.62 us
    pallas_call x1, Pallas kernels: 80.3 us -> 81.8 us  [shards(): pl.pallas_call(kernel, out_shape=(jax.ShapeDtypeStruct((32, 4, D), BF16),...]
where the time goes in v2:
time: 85.4 us; the launch traced here: 85.1 us
  Pallas kernels  81.8 us (96%)
  local copies, waits for them, and re-layouts  2.62 us (3%)
    pallas_call x1, Pallas kernels, shards(): pl.pallas_call(kernel, out_shape=(jax.ShapeDtypeStruct((32, 4, D), BF16),...  81.8 us
    unnamed x12, local copies, waits for them, and re-layouts  2.62 us

profile of v2, /device:TPU:1, one launch (start us, length us, event | category | flops | bytes accessed | tf_op | source)
XLA Modules:
  0.0 85.1 jit_solution(11730087050281172611)
XLA Ops:
  0.6 0.0 copy-start.3
  0.6 0.0 copy-start.2
  0.7 0.0 copy-start.1
  0.7 0.0 copy-start.4
  0.7 0.6 copy-done.3
  1.3 0.0 copy-done.2
  1.3 0.0 copy-done.1
  1.3 0.0 copy-done.4
  1.4 0.0 copy-start
  1.4 0.8 copy-done
  2.1 81.8 %shard_map.140 = (bf16[32,4,512]{2,1,0:T(4,128)(2,1)S(1)}, f32[1,16]{1,0:T(1,128)S(1)}) custom-call(bf16[512,512]{1,0:T(8,128)(2,1)} %bitcast.13, s32[1,512]{1,0:T(1,128)S(1)} %bitcast.8, s32[2,128]{1,0:T(2,128)S(1)} %bitcast.11, s32[16,512]{1,0:T(8,128)S(1)} %copy-done, f32[1,512]{1,0:T(1,128)S(1)} %bitcast.9, bf16[512,128]{1,0:T(8,128)(2,1)} %w_q.1, ...), custom_call_target="tpu_custom_call" | custom-call | tf_op jit(solution)/shard_map/pallas_call | solution.py:272
  84.0 0.7 copy.17
  84.6 0.5 copy.18
Async XLA Ops:
  0.6 0.7 copy-start.3
  0.6 0.7 copy-start.2
  0.7 0.7 copy-start.1
  0.7 0.7 copy-start.4
  1.4 0.8 copy-start

commit v3 on v2

--- a/solution.py
+++ b/solution.py
@@ -9,7 +9,14 @@
 BF16 = jnp.bfloat16
 MESH = pl.DeviceIdType.MESH
 EPS = 1e-6
+TURNS = (7, 6, 5, 4, 3, 2, 1, 0)
 ROUNDS, NX = 128, 4
+ORDER = (4, 3, 5, 2, 6, 1, 7, 0)
+
+
+def distance(k):
+    return 4 + (1 - 2 * lax.rem(k, 2)) * ((k + 1) // 2)
+
 D, HD, ROWS, SLOTS = 512, 128, 512, 256
 MARK = 2.0 ** 100
 DEAD = -1e30
@@ -39,31 +46,42 @@
 
 
 def kernel(
-    tokens_hbm, cells, seam, obs, gain, w_q, w_k, w_v, w_o, w_g, w_u, w_d, w_r,
+    tokens_hbm, cells_hbm, seam_hbm, obs_hbm, gain_hbm,
+    w_q, w_k, w_v, w_o, w_g, w_u, w_d, w_r_hbm,
     out, logits,
-    tokens, wqkv, wo, wg, wu, wd,
+    tokens, cells, seam, obs, gain, w_r, wqkv, wo, wg, wu, wd,
     x1, tok, normed, qkv, local, sx, sb, ra, rb, hot_t, ff, ffb, cx, cb, px, pr,
-    w_sem, r_send, r_recv, x_send, x_recv,
+    w_sem, r_send, r_recv, x_send, x_recv, t_send, t_recv, tx_send, tx_recv,
 ):
     me = lax.axis_index("round")
     m = lax.axis_index("mp")
     z, y, core = me // 16, lax.rem(me // 2, 8), lax.rem(me, 2)
 
-    def far_first(k):
-        return 4 + (1 - 2 * lax.rem(k, 2)) * ((k + 1) // 2)
-
-    def round_peer(k):
-        to_z = lax.rem(z + far_first(k // 16), 8)
-        to_y = lax.rem(y + far_first(lax.rem(k // 2, 8)), 8)
-        to_core = lax.rem(core + 1 - lax.rem(k, 2), 2)
-        return to_z * 16 + to_y * 2 + to_core
+    def z_of(k):
+        return lax.rem(z + distance(k), 8) * 16
+
+    columns = [
+        lax.rem(y + d, 8) * 2 + (c if swap else 1 - c)
+        for d in ORDER
+        for swap, c in ((False, core), (True, core))
+    ]
+
+    def each_round(act):
+        def turn(k, carry):
+            plane = z_of(k)
+            for column in columns:
+                act(plane + column, k)
+            return carry
+
+        lax.fori_loop(0, 7, turn, 0)
+        for column in columns[:15]:
+            act(z * 16 + column, 7)
 
     def x_peer(k):
         return lax.rem(m + k, NX)
 
     def send_rounds(src, dst, slot):
-        def step(k, carry):
-            to = round_peer(k)
+        def act(to, turn):
             pltpu.make_async_remote_copy(
                 src_ref=src(to),
                 dst_ref=dst.at[me],
@@ -72,9 +90,8 @@
                 device_id=(to, m),
                 device_id_type=MESH,
             ).start()
-            return carry
-
-        lax.fori_loop(0, ROUNDS - 1, step, 0)
+
+        each_round(act)
 
     def wait_rounds(buffer, sem, slot):
         others = buffer.at[pl.ds(0, ROUNDS - 1)]
@@ -100,17 +117,23 @@
         for copy in started:
             copy.wait()
 
-    load_tokens = pltpu.make_async_copy(tokens_hbm, tokens, w_sem.at[7])
-    load_tokens.start()
+    chunk = pl.ds(pl.multiple_of(m * 128, 128), 128)
+    first = [
+        pltpu.make_async_copy(cells_hbm, cells, w_sem.at[7]),
+        pltpu.make_async_copy(tokens_hbm.at[:, chunk], tokens, w_sem.at[8]),
+        pltpu.make_async_copy(seam_hbm, seam, w_sem.at[9]),
+        pltpu.make_async_copy(obs_hbm, obs, w_sem.at[10]),
+        pltpu.make_async_copy(gain_hbm, gain, w_sem.at[11]),
+        pltpu.make_async_copy(w_r_hbm, w_r, w_sem.at[12]),
+    ]
+    for load in first:
+        load.start()
     barrier = pltpu.get_barrier_semaphore()
 
-    def greet(k, carry):
-        pl.semaphore_signal(
-            barrier, inc=1, device_id=(round_peer(k), m), device_id_type=MESH
-        )
-        return carry
-
-    lax.fori_loop(0, ROUNDS - 1, greet, 0)
+    def greet(to, turn):
+        pl.semaphore_signal(barrier, inc=1, device_id=(to, m), device_id_type=MESH)
+
+    each_round(greet)
     for k in range(1, NX):
         pl.semaphore_signal(
             barrier, inc=1, device_id=(me, x_peer(k)), device_id_type=MESH
@@ -128,18 +151,30 @@
     for load in loads:
         load.start()
 
+    for load in first:
+        load.wait()
     cell_row = cells[...].astype(F32)
     diagonal = iota((128, 128), 0) == iota((128, 128), 1)
     lanes = iota((128, 512), 1)
-    load_tokens.wait()
     for b in range(4):
         part = cell_row[:, b * 128 : b * 128 + 128]
         col = jnp.sum(jnp.where(diagonal, part, 0.0), axis=1, keepdims=True)
         picked = mm(hot(lanes == col.astype(jnp.int32)), tokens[...])
-        x1[b * 32 : b * 32 + 32] = picked.astype(BF16).reshape(32, 4, D)
+        x1[b * 32 : b * 32 + 32] = picked.astype(BF16).reshape(32, 4, 128)
     pl.semaphore_wait(barrier, ROUNDS - 1 + NX - 1)
-    send_rounds(lambda i: x1.at[i], tok, 0)
-    tok[me] = x1[me]
+
+    def send_tokens(to, turn):
+        pltpu.make_async_remote_copy(
+            src_ref=x1.at[to],
+            dst_ref=tok.at[m, me],
+            send_sem=t_send,
+            recv_sem=t_recv.at[turn],
+            device_id=(to, m),
+            device_id_type=MESH,
+        ).start()
+
+    each_round(send_tokens)
+    tok[m, me] = x1[me]
     loads[6].wait()
     share_wo = send_x(lambda i: wo.at[m], wo.at[m], 0)
 
@@ -163,10 +198,31 @@
     gain_row = gain[...]
     for load in loads[:3]:
         load.wait()
-    wait_rounds(tok, r_recv, 0)
+    forwards = []
+    for k in TURNS:
+        from_z = lax.rem(z + 8 - ORDER[k], 8) * 16
+        plane = tok.at[m, pl.ds(from_z, 16)]
+        landed = plane if k < 7 else tok.at[m, pl.ds(0, 15)]
+        pltpu.make_async_copy(landed, landed, t_recv.at[k]).wait()
+        for i in (2, 1, 3):
+            copy = pltpu.make_async_remote_copy(
+                src_ref=plane,
+                dst_ref=plane,
+                send_sem=tx_send.at[k, i],
+                recv_sem=tx_recv.at[k, i],
+                device_id=(me, x_peer(i)),
+                device_id_type=MESH,
+            )
+            copy.start()
+            forwards.append(copy)
+    for copy in forwards:
+        copy.wait_recv()
 
     def norm_step(c, carry):
-        values = tok[pl.ds(c * 32, 32)].reshape(128, D).astype(F32)
+        at = pl.ds(c * 32, 32)
+        values = jnp.concatenate(
+            [tok[i, at].reshape(128, 128) for i in range(NX)], axis=1
+        ).astype(F32)
         spread = jnp.mean(values * values, axis=-1, keepdims=True)
         normal = (values * lax.rsqrt(spread + EPS) * gain_row).astype(BF16)
         at = pl.ds(pl.multiple_of(c * 128, 128), 128)
@@ -229,7 +285,9 @@
     send_rounds(lambda i: ra.at[i], rb, 2)
     rb[me] = ra[me]
 
-    own_tok = tok[pl.ds(m * 32, 32)].reshape(128, D).astype(F32)
+    own_tok = jnp.concatenate(
+        [tok[i, pl.ds(m * 32, 32)].reshape(128, 128) for i in range(NX)], axis=1
+    ).astype(F32)
     finish(share_wo)
     finish(share_ff)
     ff_own = ffb[0] + ffb[1] + ffb[2] + ffb[3]
@@ -253,8 +311,12 @@
     wait_rounds(pr, r_recv, 3)
     pooled = jnp.sum(pr[...], axis=0)
     logits[...] = (pooled / divisor)[:, 0:16]
-    for slot, buffer in enumerate((tok, sb, rb, pr)):
+    for slot, buffer in ((1, sb), (2, rb), (3, pr)):
         wait_rounds(buffer, r_send, slot)
+    sent_tokens = x1.at[pl.ds(0, ROUNDS - 1)]
+    pltpu.make_async_copy(sent_tokens, sent_tokens, t_send).wait()
+    for copy in forwards:
+        copy.wait_send()
 
 
 def in_hbm(array):
@@ -275,28 +337,35 @@
             jax.ShapeDtypeStruct((32, 4, D), BF16),
             jax.ShapeDtypeStruct((1, 16), F32),
         ),
-        in_specs=[hbm] + [vmem] * 4 + [hbm] * 7 + [vmem],
+        in_specs=[hbm] * 13,
         out_specs=(vmem, vmem),
         scratch_shapes=[
-            V((D, D), BF16), V((D, 3 * HD), BF16), V((NX, HD, D), BF16),
+            V((D, 128), BF16), V((1, 512), jnp.int32), V((2, 128), jnp.int32),
+            V((16, 512), jnp.int32), V((1, D), F32), V((1, D), F32),
+            V((D, 3 * HD), BF16), V((NX, HD, D), BF16),
             V((D, D), BF16), V((D, D), BF16), V((D, D), BF16),
-            V((ROUNDS, 4, D), BF16), V((ROUNDS, 4, D), BF16), V((ROWS, D), BF16),
+            V((ROUNDS, 4, 128), BF16), V((NX, ROUNDS, 4, 128), BF16), V((ROWS, D), BF16),
             V((ROWS, 3 * HD), BF16), V((ROWS, HD), F32),
             V((ROUNDS, 2, 3 * HD), BF16), V((ROUNDS, 2, 3 * HD), BF16),
             V((ROUNDS, 2, HD), BF16), V((ROUNDS, 2, HD), BF16),
             V((ROWS, SLOTS), BF16), V((NX, 128, D), F32), V((NX, 128, D), F32),
             V((NX, 128, HD), BF16), V((NX, 128, HD), BF16),
             V((NX, 1, 128), F32), V((ROUNDS, 1, 128), F32),
-            dma((8,)), dma((4,)), dma((4,)), dma((4, NX)), dma((4, NX)),
+            dma((13,)), dma((4,)), dma((4,)), dma((4, NX)), dma((4, NX)),
+            dma, dma((8,)), dma((8, NX)), dma((8, NX)),
         ],
         compiler_params=pltpu.CompilerParams(
             collective_id=0, has_side_effects=True, vmem_limit_bytes=40 * 2 ** 20
         ),
     )(
-        in_hbm(tokens.reshape(512, D)), cell_order.reshape(1, 512), seam_rows[0].T,
-        obs_mask, norm_gain.reshape(1, D),
-        *[in_hbm(w) for w in (w_query, w_key, w_value, w_out, w_gate, w_up, w_down)],
-        w_read.reshape(1, D),
+        *[
+            in_hbm(array)
+            for array in (
+                tokens.reshape(512, D), cell_order.reshape(1, 512), seam_rows[0].T,
+                obs_mask, norm_gain.reshape(1, D), w_query, w_key, w_value, w_out,
+                w_gate, w_up, w_down, w_read.reshape(1, D),
+            )
+        ]
     )
     return out, logits.reshape(16)
 

time: 85.4 us -> 68 us (0.80)
  Pallas kernels: 81.8 us -> 66.1 us
  local copies, waits for them, and re-layouts: 2.62 us -> 1.17 us
    pallas_call x1, Pallas kernels: 81.8 us -> 66.1 us  [shards(): pl.pallas_call(kernel, out_shape=(jax.ShapeDtypeStruct((32, 4, D), BF16),...]
    unnamed x12 -> x2, local copies, waits for them, and re-layouts: 2.62 us -> 1.17 us
where the time goes in v3:
time: 68 us; the launch traced here: 67.9 us
  Pallas kernels  66.1 us (97%)
  local copies, waits for them, and re-layouts  1.17 us (2%)
    pallas_call x1, Pallas kernels, shards(): pl.pallas_call(kernel, out_shape=(jax.ShapeDtypeStruct((32, 4, D), BF16),...  66.1 us

profile of v3, /device:TPU:1, one launch (start us, length us, event | category | flops | bytes accessed | tf_op | source)
XLA Modules:
  0.0 67.9 jit_solution(1053301188266255179)
XLA Ops:
  0.6 66.1 %shard_map.140 = (bf16[32,4,512]{2,1,0:T(4,128)(2,1)S(1)}, f32[1,16]{1,0:T(1,128)S(1)}) custom-call(bf16[512,512]{1,0:T(8,128)(2,1)} %bitcast.9, s32[1,512]{1,0:T(1,128)} %bitcast.10, s32[2,128]{1,0:T(2,128)} %bitcast.13, s32[16,512]{1,0:T(8,128)} %obs_hbm.1, f32[1,512]{1,0:T(1,128)} %bitcast.11, bf16[512,128]{1,0:T(8,128)(2,1)} %w_q.1, ...), custom_call_target="tpu_custom_call" | custom-call | tf_op jit(solution)/shard_map/pallas_call | solution.py:334
  66.7 0.7 copy.17
  67.4 0.5 copy.18

commit v4 on v3

--- a/solution.py
+++ b/solution.py
@@ -51,7 +51,7 @@
     out, logits,
     tokens, cells, seam, obs, gain, w_r, wqkv, wo, wg, wu, wd,
     x1, tok, normed, qkv, local, sx, sb, ra, rb, hot_t, ff, ffb, cx, cb, px, pr,
-    w_sem, r_send, r_recv, x_send, x_recv, t_send, t_recv, tx_send, tx_recv,
+    w_sem, r_send, r_recv, x_send, x_recv, p_send, p_recv, t_send, t_recv, tx_send, tx_recv,
 ):
     me = lax.axis_index("round")
     m = lax.axis_index("mp")
@@ -79,6 +79,9 @@
 
     def x_peer(k):
         return lax.rem(m + k, NX)
+
+    def near_peer(k):
+        return me + (1 - 2 * core) * (k % 2), x_peer(k // 2)
 
     def send_rounds(src, dst, slot):
         def act(to, turn):
@@ -126,18 +129,19 @@
         pltpu.make_async_copy(gain_hbm, gain, w_sem.at[11]),
         pltpu.make_async_copy(w_r_hbm, w_r, w_sem.at[12]),
     ]
+    barrier = pltpu.get_barrier_semaphore()
+
+    def greet(to, turn):
+        pl.semaphore_signal(barrier, inc=1, device_id=(to, m), device_id_type=MESH)
+
+    each_round(greet)
+    for k in range(2, 8):
+        pl.semaphore_signal(
+            barrier, inc=1, device_id=near_peer(k), device_id_type=MESH
+        )
+
     for load in first:
         load.start()
-    barrier = pltpu.get_barrier_semaphore()
-
-    def greet(to, turn):
-        pl.semaphore_signal(barrier, inc=1, device_id=(to, m), device_id_type=MESH)
-
-    each_round(greet)
-    for k in range(1, NX):
-        pl.semaphore_signal(
-            barrier, inc=1, device_id=(me, x_peer(k)), device_id_type=MESH
-        )
 
     loads = [
         pltpu.make_async_copy(w_q, wqkv.at[:, pl.ds(0, HD)], w_sem.at[0]),
@@ -161,7 +165,7 @@
         col = jnp.sum(jnp.where(diagonal, part, 0.0), axis=1, keepdims=True)
         picked = mm(hot(lanes == col.astype(jnp.int32)), tokens[...])
         x1[b * 32 : b * 32 + 32] = picked.astype(BF16).reshape(32, 4, 128)
-    pl.semaphore_wait(barrier, ROUNDS - 1 + NX - 1)
+    pl.semaphore_wait(barrier, ROUNDS - 1 + 6)
 
     def send_tokens(to, turn):
         pltpu.make_async_remote_copy(
@@ -215,22 +219,18 @@
             )
             copy.start()
             forwards.append(copy)
-    for copy in forwards:
-        copy.wait_recv()
-
-    def norm_step(c, carry):
-        at = pl.ds(c * 32, 32)
+    for n, k in enumerate(TURNS):
+        for copy in forwards[3 * n : 3 * n + 3]:
+            copy.wait_recv()
+        from_z = lax.rem(z + 8 - ORDER[k], 8)
+        at = pl.ds(from_z * 16, 16)
         values = jnp.concatenate(
-            [tok[i, at].reshape(128, 128) for i in range(NX)], axis=1
+            [tok[i, at].reshape(64, 128) for i in range(NX)], axis=1
         ).astype(F32)
         spread = jnp.mean(values * values, axis=-1, keepdims=True)
         normal = (values * lax.rsqrt(spread + EPS) * gain_row).astype(BF16)
-        at = pl.ds(pl.multiple_of(c * 128, 128), 128)
-        normed[at, :] = normal
-        qkv[at, :] = mm(normal, wqkv[...]).astype(BF16)
-        return carry
-
-    lax.fori_loop(0, 4, norm_step, 0)
+        normed[pl.ds(pl.multiple_of(from_z * 64, 64), 64), :] = normal
+    qkv[...] = mm(normed[...], wqkv[...]).astype(BF16)
 
     sent = mm(hot_g, qkv[...])
     sent = jnp.where((iota((SLOTS, 3 * HD), 1) == 0) & empty, MARK, sent).astype(BF16)
@@ -303,18 +303,53 @@
     out[...] = result.reshape(32, 4, D)
 
     dots = jnp.sum(result.astype(F32) * w_r[...], axis=1, keepdims=True)
-    px[m] = jnp.sum(support * dots, axis=0, keepdims=True)
-    sum_x = send_x(lambda i: px.at[m], px.at[m], 3)
-    finish(sum_x)
-    pr[me] = jnp.sum(px[...], axis=0)
-    send_rounds(lambda i: pr.at[me], pr, 3)
-    wait_rounds(pr, r_recv, 3)
+    px[2 * m + core] = jnp.sum(support * dots, axis=0, keepdims=True)
+    sums = []
+    for k in range(1, 8):
+        copy = pltpu.make_async_remote_copy(
+            src_ref=px.at[2 * m + core],
+            dst_ref=px.at[2 * m + core],
+            send_sem=p_send.at[k],
+            recv_sem=p_recv.at[k],
+            device_id=near_peer(k),
+            device_id_type=MESH,
+        )
+        copy.start()
+        sums.append(copy)
+    finish(sums)
+    chip = z * 8 + y
+    pr[chip] = jnp.sum(px[...], axis=0)
+
+    def send_sum(plane, column):
+        pltpu.make_async_remote_copy(
+            src_ref=pr.at[chip],
+            dst_ref=pr.at[chip],
+            send_sem=r_send.at[3],
+            recv_sem=r_recv.at[3],
+            device_id=(plane + column, m),
+            device_id_type=MESH,
+        ).start()
+
+    same_core = columns[1::2]
+
+    def sum_turn(k, carry):
+        plane = z_of(k)
+        for column in same_core:
+            send_sum(plane, column)
+        return carry
+
+    lax.fori_loop(0, 7, sum_turn, 0)
+    for column in same_core[:7]:
+        send_sum(z * 16, column)
+    others = pr.at[pl.ds(0, 63)]
+    pltpu.make_async_copy(others, others, r_recv.at[3]).wait()
     pooled = jnp.sum(pr[...], axis=0)
     logits[...] = (pooled / divisor)[:, 0:16]
-    for slot, buffer in ((1, sb), (2, rb), (3, pr)):
+    for slot, buffer in ((1, sb), (2, rb)):
         wait_rounds(buffer, r_send, slot)
     sent_tokens = x1.at[pl.ds(0, ROUNDS - 1)]
     pltpu.make_async_copy(sent_tokens, sent_tokens, t_send).wait()
+    pltpu.make_async_copy(others, others, r_send.at[3]).wait()
     for copy in forwards:
         copy.wait_send()
 
@@ -350,8 +385,9 @@
             V((ROUNDS, 2, HD), BF16), V((ROUNDS, 2, HD), BF16),
             V((ROWS, SLOTS), BF16), V((NX, 128, D), F32), V((NX, 128, D), F32),
             V((NX, 128, HD), BF16), V((NX, 128, HD), BF16),
-            V((NX, 1, 128), F32), V((ROUNDS, 1, 128), F32),
-            dma((13,)), dma((4,)), dma((4,)), dma((4, NX)), dma((4, NX)),
+            V((8, 1, 128), F32), V((64, 1, 128), F32),
+            dma((13,)), dma((4,)), dma((4,)), dma((3, NX)), dma((3, NX)),
+            dma((8,)), dma((8,)),
             dma, dma((8,)), dma((8, NX)), dma((8, NX)),
         ],
         compiler_params=pltpu.CompilerParams(

time: 68 us -> 66.3 us (0.975)
  Pallas kernels: 66.1 us -> 64.4 us
    pallas_call x1, Pallas kernels: 66.1 us -> 64.4 us  [shards(): pl.pallas_call(kernel, out_shape=(jax.ShapeDtypeStruct((32, 4, D), BF16),...]
where the time goes in v4:
time: 66.3 us; the launch traced here: 66.2 us
  Pallas kernels  64.4 us (97%)
  local copies, waits for them, and re-layouts  1.17 us (2%)
    pallas_call x1, Pallas kernels, shards(): pl.pallas_call(kernel, out_shape=(jax.ShapeDtypeStruct((32, 4, D), BF16),...  64.4 us

profile of v4, /device:TPU:1, one launch (start us, length us, event | category | flops | bytes accessed | tf_op | source)
XLA Modules:
  0.0 66.2 jit_solution(2114757216388027041)
XLA Ops:
  0.6 64.4 %shard_map.140 = (bf16[32,4,512]{2,1,0:T(4,128)(2,1)S(1)}, f32[1,16]{1,0:T(1,128)S(1)}) custom-call(bf16[512,512]{1,0:T(8,128)(2,1)} %bitcast.9, s32[1,512]{1,0:T(1,128)} %bitcast.10, s32[2,128]{1,0:T(2,128)} %bitcast.13, s32[16,512]{1,0:T(8,128)} %obs_hbm.1, f32[1,512]{1,0:T(1,128)} %bitcast.11, bf16[512,128]{1,0:T(8,128)(2,1)} %w_q.1, ...), custom_call_target="tpu_custom_call" | custom-call | tf_op jit(solution)/shard_map/pallas_call | solution.py:369
  65.0 0.7 copy.17
  65.7 0.5 copy.18

commit v5 on v4

--- a/solution.py
+++ b/solution.py
@@ -177,7 +177,16 @@
             device_id_type=MESH,
         ).start()
 
-    each_round(send_tokens)
+    for column in columns[:15]:
+        send_tokens(z * 16 + column, 7)
+
+    def token_turn(i, carry):
+        plane = z_of(6 - i)
+        for column in columns:
+            send_tokens(plane + column, 6 - i)
+        return carry
+
+    lax.fori_loop(0, 7, token_turn, 0)
     tok[m, me] = x1[me]
     loads[6].wait()
     share_wo = send_x(lambda i: wo.at[m], wo.at[m], 0)
@@ -288,9 +297,8 @@
     own_tok = jnp.concatenate(
         [tok[i, pl.ds(m * 32, 32)].reshape(128, 128) for i in range(NX)], axis=1
     ).astype(F32)
-    finish(share_wo)
     finish(share_ff)
-    ff_own = ffb[0] + ffb[1] + ffb[2] + ffb[3]
+    base = own_tok + (ffb[0] + ffb[1] + ffb[2] + ffb[3])
     wait_rounds(rb, r_recv, 2)
 
     both = local[...] + mm(hot_t[...], rb[...].reshape(SLOTS, HD))
@@ -298,8 +306,9 @@
     comb_x = send_x(lambda i: cx.at[i], cb.at[m], 2)
     cb[m] = cx[m]
     finish(comb_x)
+    finish(share_wo)
     attn = mm(cb[0], wo[0]) + mm(cb[1], wo[1]) + mm(cb[2], wo[2]) + mm(cb[3], wo[3])
-    result = (own_tok + (attn + ff_own)).astype(BF16)
+    result = (base + attn).astype(BF16)
     out[...] = result.reshape(32, 4, D)
 
     dots = jnp.sum(result.astype(F32) * w_r[...], axis=1, keepdims=True)

time: 66.3 us -> 65.3 us (0.985)
  Pallas kernels: 64.4 us -> 63.4 us
    pallas_call x1, Pallas kernels: 64.4 us -> 63.4 us  [shards(): pl.pallas_call(kernel, out_shape=(jax.ShapeDtypeStruct((32, 4, D), BF16),...]
where the time goes in v5:
time: 65.3 us; the launch traced here: 65.2 us
  Pallas kernels  63.4 us (97%)
  local copies, waits for them, and re-layouts  1.17 us (2%)
    pallas_call x1, Pallas kernels, shards(): pl.pallas_call(kernel, out_shape=(jax.ShapeDtypeStruct((32, 4, D), BF16),...  63.4 us

profile of v5, /device:TPU:1, one launch (start us, length us, event | category | flops | bytes accessed | tf_op | source)
XLA Modules:
  0.0 65.2 jit_solution(1325434883043861321)
XLA Ops:
  0.6 63.4 %shard_map.140 = (bf16[32,4,512]{2,1,0:T(4,128)(2,1)S(1)}, f32[1,16]{1,0:T(1,128)S(1)}) custom-call(bf16[512,512]{1,0:T(8,128)(2,1)} %bitcast.9, s32[1,512]{1,0:T(1,128)} %bitcast.10, s32[2,128]{1,0:T(2,128)} %bitcast.13, s32[16,512]{1,0:T(8,128)} %obs_hbm.1, f32[1,512]{1,0:T(1,128)} %bitcast.11, bf16[512,128]{1,0:T(8,128)(2,1)} %w_q.1, ...), custom_call_target="tpu_custom_call" | custom-call | tf_op jit(solution)/shard_map/pallas_call | solution.py:378
  64.0 0.7 %copy.17 = bf16[32,4,512]{2,1,0:T(4,128)(2,1)} copy(bf16[32,4,512]{2,1,0:T(4,128)(2,1)S(1)} %get-tuple-element.8) | data formatting | bytes 262144
  64.7 0.5 copy.18

commit v6 on v5

--- a/solution.py
+++ b/solution.py
@@ -238,8 +238,9 @@
         ).astype(F32)
         spread = jnp.mean(values * values, axis=-1, keepdims=True)
         normal = (values * lax.rsqrt(spread + EPS) * gain_row).astype(BF16)
-        normed[pl.ds(pl.multiple_of(from_z * 64, 64), 64), :] = normal
-    qkv[...] = mm(normed[...], wqkv[...]).astype(BF16)
+        here = pl.ds(pl.multiple_of(from_z * 64, 64), 64)
+        normed[here, :] = normal
+        qkv[here, :] = mm(normal, wqkv[...]).astype(BF16)
 
     sent = mm(hot_g, qkv[...])
     sent = jnp.where((iota((SLOTS, 3 * HD), 1) == 0) & empty, MARK, sent).astype(BF16)
@@ -314,7 +315,7 @@
     dots = jnp.sum(result.astype(F32) * w_r[...], axis=1, keepdims=True)
     px[2 * m + core] = jnp.sum(support * dots, axis=0, keepdims=True)
     sums = []
-    for k in range(1, 8):
+    for k in (4, 5, 2, 3, 6, 7, 1):
         copy = pltpu.make_async_remote_copy(
             src_ref=px.at[2 * m + core],
             dst_ref=px.at[2 * m + core],

time: 65.3 us -> 65.2 us (level)
  no operation moved by 1% of the time
where the time goes in v6:
time: 65.2 us; the launch traced here: 65 us
  Pallas kernels  63.2 us (97%)
  local copies, waits for them, and re-layouts  1.17 us (2%)
    pallas_call x1, Pallas kernels, shards(): pl.pallas_call(kernel, out_shape=(jax.ShapeDtypeStruct((32, 4, D), BF16),...  63.2 us

profile of v6, /device:TPU:1, one launch (start us, length us, event | category | flops | bytes accessed | tf_op | source)
XLA Modules:
  0.0 65.0 jit_solution(2472838754746284157)
XLA Ops:
  0.6 63.2 %shard_map.140 = (bf16[32,4,512]{2,1,0:T(4,128)(2,1)S(1)}, f32[1,16]{1,0:T(1,128)S(1)}) custom-call(bf16[512,512]{1,0:T(8,128)(2,1)} %bitcast.9, s32[1,512]{1,0:T(1,128)} %bitcast.10, s32[2,128]{1,0:T(2,128)} %bitcast.13, s32[16,512]{1,0:T(8,128)} %obs_hbm.1, f32[1,512]{1,0:T(1,128)} %bitcast.11, bf16[512,128]{1,0:T(8,128)(2,1)} %w_q.1, ...), custom_call_target="tpu_custom_call" | custom-call | tf_op jit(solution)/shard_map/pallas_call | solution.py:379
  63.9 0.7 %copy.17 = bf16[32,4,512]{2,1,0:T(4,128)(2,1)} copy(bf16[32,4,512]{2,1,0:T(4,128)(2,1)S(1)} %get-tuple-element.8) | data formatting | bytes 262144
  64.5 0.5 copy.18
